TPU v7x, 256 devices: a whole 4x4x8 slice. The times are simulated.
256 devices in a mesh: dp: 16 (over x, y_hi, core), tensor: 16 (over y_lo, z).
Axes of the slice: x: 4, y: 4 (y_hi: 2, y_lo: 2; y = y_hi * 2 + y_lo), z: 8, core: 2. Of those that a mesh axis runs over, the one named last changes fastest.
Arguments:
- inputs: bfloat16 [8192, 6144], P(('dp', 'tensor')), may hold values from -36 to 36
- gain: float32 [6144], replicated, may hold values from 0.25 to 1.75
- w_in: bfloat16 [6144, 12288], P(None, 'tensor'), may hold values from -0.078125 to 0.078125
- grad_act: bfloat16 [8192, 12288], P('dp', 'tensor'), may hold values from -6 to 6
- residual_gradient: bfloat16 [8192, 6144], P(('dp', 'tensor')), may hold values from -6 to 6
Outputs:
- block_input_gradient: bfloat16 [8192, 6144], P(('dp', 'tensor'))
- grad_w: float32 [6144, 12288], P('dp', 'tensor')
- scale_gradient: float32 [6144], replicated
All inputs are finite; a program needn't handle non-finite values.
Results may differ from a plain program's by a relative error of at most 0.022.
Values may be sent and summed in bfloat16 or wider, within the bound.
No kernel may reach another device: no remote copies, remote signals or barrier semaphores. Data moves between devices by JAX's collectives and lax.ppermute only.
A program may use at most 128 MiB of HBM per device.

v0:
```python
import jax
import jax.numpy as jnp
from jax import lax
from jax.sharding import PartitionSpec as P


def contract_rows(left, right):
    return lax.dot_general(
        left, right, (((0,), (0,)), ((), ())), preferred_element_type=jnp.float32
    )


def on_device(inputs, gain, w_in, grad_act, residual_gradient):
    values = inputs.astype(jnp.float32)
    centered_input = values - jnp.mean(values, axis=1, keepdims=True)
    inverse_deviation = lax.rsqrt(
        jnp.mean(centered_input * centered_input, axis=1, keepdims=True) + 1e-06
    )
    standardized_input = centered_input * inverse_deviation
    normed_output = (standardized_input * gain).astype(jnp.bfloat16)
    replicas = lax.axis_size("dp")
    full = lax.all_gather(normed_output, "tensor", axis=0, tiled=True)
    pre = jnp.dot(full, w_in, preferred_element_type=jnp.float32)
    unused, pullback = jax.vjp(jax.nn.gelu, pre)
    dpre = pullback(grad_act.astype(jnp.float32))[0].astype(jnp.bfloat16)
    normed_gradient = lax.psum_scatter(
        lax.dot_general(
            dpre, w_in, (((1,), (1,)), ((), ())), preferred_element_type=jnp.float32
        ).astype(jnp.bfloat16),
        "tensor",
        scatter_dimension=0,
        tiled=True,
    ).astype(jnp.float32)
    scale_terms = jnp.sum(normed_gradient * standardized_input, axis=0)
    scale_gradient = lax.psum(scale_terms, ("dp", "tensor")) / replicas
    scaled_gradient = normed_gradient * gain
    first_average = jnp.mean(scaled_gradient, axis=1, keepdims=True)
    second_average = jnp.mean(scaled_gradient * standardized_input, axis=1, keepdims=True)
    block_input_gradient = (
        residual_gradient.astype(jnp.float32)
        + inverse_deviation
        * (scaled_gradient - first_average - standardized_input * second_average)
    ).astype(jnp.bfloat16)
    term = contract_rows(full, dpre)
    grad_w = (
        lax.psum_scatter(term.astype(jnp.bfloat16), "dp", scatter_dimension=0, tiled=True).astype(
            jnp.float32
        )
        / replicas
    )
    return (block_input_gradient, grad_w, scale_gradient)


def solution(mesh):
    return jax.shard_map(
        on_device,
        mesh=mesh,
        in_specs=(
            P(("dp", "tensor"), None),
            P(),
            P(None, "tensor"),
            P("dp", "tensor"),
            P(("dp", "tensor"), None),
        ),
        out_specs=(P(("dp", "tensor"), None), P("dp", "tensor"), P()),
        check_vma=False,
    )
```

profile of v0, /device:TPU:2, one launch (start us, length us, event | category | flops | bytes accessed | tf_op | source)
XLA Modules:
  0.0 327.8 jit_solution(12556771568084619879)
XLA Ops:
  7.2 0.0 all-gather.2.cloned.1.call-start
  7.2 1.2 convert_reduce_fusion
  8.4 1.3 fusion.24
  9.7 1.9 fusion.19
  11.6 0.0 all-gather.2.cloned.1.call-update
  11.6 0.0 copy-start.3
  11.6 0.0 reduce-scatter.3.cloned.1.call-start
  11.7 85.2 %all-gather.2.cloned.1.call-done = bf16[512,6144]{1,0:T(8,128)(2,1)} async-done(((bf16[32,6144]{1,0:T(8,128)(2,1)}), bf16[512,6144]{1,0:T(8,128)(2,1)}) %all-gather.2.cloned.1.call-update) | async-done | bytes 6291472 | tf_op jit(solution)/shard_map/all_gather | solution.py:22
  96.9 9.4 %fusion.51 = f32[512,768]{1,0:T(8,128)S(1)} fusion(bf16[512,6144]{1,0:T(8,128)(2,1)} %all-gather.2.cloned.1.call-done, bf16[6144,768]{1,0:T(8,128)(2,1)} %param.7), kind=kOutput, calls=%fused_computation.65 | convolution fusion | flops 4831838208 | bytes 17301504 | tf_op jit(solution)/shard_map/dot_general | solution.py:23
  106.3 0.0 copy-done.3
  106.3 11.4 %convolution_convert_fusion.1 = bf16[512,6144]{1,0:T(8,128)(2,1)} fusion(bf16[6144,768]{1,0:T(8,128)(2,1)} %param.7, bf16[512,768]{1,0:T(8,128)(2,1)S(1)} %copy-done.3, f32[512,768]{1,0:T(8,128)S(1)} %fusion.51), kind=kOutput, calls=%fused_computation.1 | convolution fusion | flops 4843241472 | bytes 18087936 | tf_op jit(solution)/shard_map/dot_general | solution.py:27
  117.7 0.0 reduce-scatter.3.cloned.1.call-update
  117.7 0.0 reduce-scatter.5.cloned.1.call-start
  117.8 11.3 %convolution_convert_fusion = bf16[6144,768]{1,0:T(8,128)(2,1)} fusion(bf16[512,6144]{1,0:T(8,128)(2,1)} %all-gather.2.cloned.1.call-done, bf16[512,768]{1,0:T(8,128)(2,1)S(1)} %copy-done.3, f32[512,768]{1,0:T(8,128)S(1)} %fusion.51), kind=kOutput, calls=%fused_computation | convolution fusion | flops 4844814336 | bytes 18087936 | tf_op jit(solution)/shard_map/dot_general | solution.py:8
  129.0 0.0 copy-start
  129.0 0.0 copy-start.2
  129.0 0.0 copy-start.1
  129.0 0.0 reduce-scatter.5.cloned.1.call-update
  129.1 73.0 %reduce-scatter.3.cloned.1.call-done = bf16[32,6144]{1,0:T(8,128)(2,1)} async-done(((bf16[512,6144]{1,0:T(8,128)(2,1)}), bf16[32,6144]{1,0:T(8,128)(2,1)}) %reduce-scatter.3.cloned.1.call-update) | async-done | bytes 393232 | tf_op jit(solution)/shard_map/reduce_scatter | solution.py:26
  202.1 0.0 copy-done
  202.1 0.0 copy-done.2
  202.1 1.5 fusion.26
  203.6 83.6 %psum.7 = f32[6144]{0:T(1024)S(1)} all-reduce(f32[6144]{0:T(1024)S(1)} %get-tuple-element.3), channel_id=1, replica_groups=mesh['dp'=16,'tensor'=16] {'dp','tensor'}, use_global_device_ids=true, to_apply=%region_7.0 | all-reduce | flops 6144 | bytes 49152 | tf_op jit(solution)/shard_map/psum | solution.py:35
  287.1 0.6 broadcast_multiply_fusion
  287.8 0.0 copy-done.1
  287.8 2.1 fusion.23
  289.9 29.3 %reduce-scatter.5.cloned.1.call-done = bf16[384,768]{1,0:T(8,128)(2,1)} async-done(((bf16[6144,768]{1,0:T(8,128)(2,1)}), bf16[384,768]{1,0:T(8,128)(2,1)}) %reduce-scatter.5.cloned.1.call-update) | async-done | bytes 589840 | tf_op jit(solution)/shard_map/reduce_scatter | solution.py:46
  319.2 2.2 convert_multiply_fusion.2
  (3 shorter events, 0.0 us)
Async XLA Ops:
  7.2 89.8 %all-gather.2.cloned.1.call-start = ((), (), s32[]{:S(2)}) async-start(), calls=%async_computation.2 | async-start | bytes 6684672 | tf_op jit(solution)/shard_map/all_gather | solution.py:22
  11.6 94.7 %copy-start.3 = (bf16[512,768]{1,0:T(8,128)(2,1)S(1)}, bf16[512,768]{1,0:T(8,128)(2,1)}, u32[]{:S(2)}) copy-start(bf16[512,768]{1,0:T(8,128)(2,1)} %param.8) | copy-start | bytes 2359300
  11.6 190.5 %reduce-scatter.3.cloned.1.call-start = ((), (), s32[]{:S(2)}) async-start(), calls=%async_computation.3 | async-start | bytes 6684672 | tf_op jit(solution)/shard_map/reduce_scatter | solution.py:26
  117.7 201.4 %reduce-scatter.5.cloned.1.call-start = ((), (), s32[]{:S(2)}) async-start(), calls=%async_computation.4 | async-start | bytes 10027008 | tf_op jit(solution)/shard_map/reduce_scatter | solution.py:46
  129.0 73.1 %copy-start = (bf16[32,6144]{1,0:T(8,128)(2,1)S(1)}, bf16[32,6144]{1,0:T(8,128)(2,1)}, u32[]{:S(2)}) copy-start(bf16[32,6144]{1,0:T(8,128)(2,1)} %param.5) | copy-start | bytes 1179652
  129.0 73.1 %copy-start.2 = (f32[6144]{0:T(1024)S(1)}, f32[6144]{0:T(1024)}, u32[]{:S(2)}) copy-start(f32[6144]{0:T(1024)} %param.6) | copy-start | bytes 73732
  129.0 158.7 %copy-start.1 = (bf16[32,6144]{1,0:T(8,128)(2,1)S(1)}, bf16[32,6144]{1,0:T(8,128)(2,1)}, u32[]{:S(2)}) copy-start(bf16[32,6144]{1,0:T(8,128)(2,1)} %param.9) | copy-start | bytes 1179652
Sparse Core Ops, SparseCore 0:
  11.7 85.1 all-gather.1
  117.8 84.2 reduce-scatter.2
  206.8 112.2 reduce-scatter.4
where the time goes:
time: 328 us
  waiting for transfers between devices  188 us (57%)
  blocking collectives  83.6 us (25%)
  matrix products  32 us (10%)
  between operations  13.8 us (4%)
  other arithmetic  10.7 us (3%)
    all_gather x1, waiting for transfers between devices, on_device(): full = lax.all_gather(normed_output, 'tensor', axis=0, tiled=True)  85.2 us
    psum x1, blocking collectives, on_device(): scale_gradient = lax.psum(scale_terms, ('dp', 'tensor')) / replicas  83.6 us
    reduce_scatter x1, waiting for transfers between devices, on_device(): lax.psum_scatter(lax.dot_general(dpre, w_in, (((1,), (1,)), ((), ())), pr...  73 us
    reduce_scatter x1, waiting for transfers between devices, on_device(): lax.psum_scatter(term.astype(jnp.bfloat16), 'dp', scatter_dimension=0, ti...  29.3 us
    dot_general x1, matrix products, on_device(): lax.dot_general(dpre, w_in, (((1,), (1,)), ((), ())), preferred_element_t...  11.4 us
    dot_general x1, matrix products, contract_rows(): lax.dot_general(left, right, (((0,), (0,)), ((), ())), preferred_element_...  11.3 us
    dot_general x1, matrix products, on_device(): pre = jnp.dot(full, w_in, preferred_element_type=jnp.float32)  9.35 us
  transfers between devices with their start and end apart: 3, of which 3 were waited for; matrix products, arithmetic and copies ran while one was open for 5% of the time, Pallas kernels for 0%

commit v1 on v0

--- a/solution.py
+++ b/solution.py
@@ -19,7 +19,9 @@
     standardized_input = centered_input * inverse_deviation
     normed_output = (standardized_input * gain).astype(jnp.bfloat16)
     replicas = lax.axis_size("dp")
-    full = lax.all_gather(normed_output, "tensor", axis=0, tiled=True)
+    full = jnp.concatenate(
+        lax.all_to_all(jnp.stack([normed_output] * lax.axis_size("tensor")), "tensor", 0, 0), axis=0
+    )
     pre = jnp.dot(full, w_in, preferred_element_type=jnp.float32)
     unused, pullback = jax.vjp(jax.nn.gelu, pre)
     dpre = pullback(grad_act.astype(jnp.float32))[0].astype(jnp.bfloat16)

time: 328 us -> 388 us (1.18)
  blocking collectives: 83.6 us -> 232 us
  waiting for transfers between devices: 188 us -> 103 us
  matrix products: 32 us -> 24.9 us
    all_to_all x0 -> x1, blocking collectives: none -> 149 us  [on_device(): lax.all_to_all(jnp.stack([normed_output] * lax.axis_size('tensor')), 'ten...]
    all_gather x1 -> x0, waiting for transfers between devices: 85.2 us -> none  [on_device(): full = lax.all_gather(normed_output, 'tensor', axis=0, tiled=True)]
    dot_general x1, matrix products: 9.35 us -> 5.06 us  [on_device(): pre = jnp.dot(full, w_in, preferred_element_type=jnp.float32)]
  transfers between devices with their start and end apart: 3 -> 2, of which waited for: 3 -> 2; matrix products, arithmetic and copies ran while one was open for 5% -> 4% of each run, Pallas kernels for 0% -> 0%
where the time goes in v1:
time: 388 us
  blocking collectives  232 us (60%)
  waiting for transfers between devices  103 us (27%)
  matrix products  24.9 us (6%)
  between operations  14.1 us (4%)
  other arithmetic  9.94 us (3%)
    all_to_all x1, blocking collectives, on_device(): lax.all_to_all(jnp.stack([normed_output] * lax.axis_size('tensor')), 'ten...  149 us
    psum x1, blocking collectives, on_device(): scale_gradient = lax.psum(scale_terms, ('dp', 'tensor')) / replicas  83.1 us
    reduce_scatter x1, waiting for transfers between devices, on_device(): lax.psum_scatter(lax.dot_general(dpre, w_in, (((1,), (1,)), ((), ())), pr...  73.7 us
    reduce_scatter x1, waiting for transfers between devices, on_device(): lax.psum_scatter(term.astype(jnp.bfloat16), 'dp', scatter_dimension=0, ti...  29.7 us
    dot_general x1, matrix products, contract_rows(): lax.dot_general(left, right, (((0,), (0,)), ((), ())), preferred_element_...  11.3 us
    dot_general x1, matrix products, on_device(): lax.dot_general(dpre, w_in, (((1,), (1,)), ((), ())), preferred_element_t...  8.52 us
  transfers between devices with their start and end apart: 2, of which 2 were waited for; matrix products, arithmetic and copies ran while one was open for 4% of the time, Pallas kernels for 0%

profile of v1, /device:TPU:2, one launch (start us, length us, event | category | flops | bytes accessed | tf_op | source)
XLA Modules:
  0.0 387.9 jit_solution(17176431420358329965)
XLA Ops:
  7.2 0.0 reduce-scatter.3.cloned.1.call-start
  7.2 1.2 convert_reduce_fusion
  8.4 1.3 fusion.24
  9.7 1.2 fusion.19
  10.9 0.0 slice-start
  10.9 0.0 slice-start.1
  10.9 0.8 stack.2
  11.6 0.0 slice-start.2
  11.7 148.9 %all_to_all.5 = bf16[16,32,6144]{2,1,0:T(8,128)(2,1)S(1)} all-to-all(bf16[16,32,6144]{2,1,0:T(8,128)(2,1)S(1)} %stack.2), channel_id=1, replica_groups=mesh['dp'=16,'tensor'=16] {'tensor'}, dimensions={0} | all-to-all | bytes 12582912 | tf_op jit(solution)/shard_map/all_to_all | solution.py:23
  160.6 0.0 copy-start.1
  160.6 2.6 copy-done.1
  163.2 0.0 slice-done
  163.2 0.0 slice-done.1
  163.2 0.0 slice-done.2
  163.2 0.0 copy-start.4
  163.2 5.1 %fusion.51 = f32[512,768]{1,0:T(8,128)S(1)} fusion(bf16[512,6144]{1,0:T(8,128)(2,1)S(1)} %bitcast.5, bf16[6144,768]{1,0:T(8,128)(2,1)S(1)} %bitcast.8), kind=kOutput, calls=%fused_computation.65 | convolution fusion | flops 4831838208 | bytes 17301504 | tf_op jit(solution)/shard_map/dot_general | solution.py:25
  168.3 0.0 copy-done.4
  168.3 8.5 %convolution_convert_fusion.1 = bf16[512,6144]{1,0:T(8,128)(2,1)} fusion(bf16[6144,768]{1,0:T(8,128)(2,1)S(1)} %bitcast.8, bf16[512,768]{1,0:T(8,128)(2,1)S(1)} %copy-done.4, f32[512,768]{1,0:T(8,128)S(1)} %fusion.51), kind=kOutput, calls=%fused_computation.1 | convolution fusion | flops 4843241472 | bytes 18087936 | tf_op jit(solution)/shard_map/dot_general | solution.py:29
  176.8 0.0 reduce-scatter.3.cloned.1.call-update
  176.9 0.0 reduce-scatter.5.cloned.1.call-start
  176.9 11.3 %convolution_convert_fusion = bf16[6144,768]{1,0:T(8,128)(2,1)} fusion(bf16[512,6144]{1,0:T(8,128)(2,1)} %bitcast.6, bf16[512,768]{1,0:T(8,128)(2,1)S(1)} %copy-done.4, f32[512,768]{1,0:T(8,128)S(1)} %fusion.51), kind=kOutput, calls=%fused_computation | convolution fusion | flops 4844814336 | bytes 18087936 | tf_op jit(solution)/shard_map/dot_general | solution.py:8
  188.2 0.0 copy-start
  188.2 0.0 copy-start.3
  188.2 0.0 copy-start.2
  188.2 0.0 reduce-scatter.5.cloned.1.call-update
  188.2 73.7 %reduce-scatter.3.cloned.1.call-done = bf16[32,6144]{1,0:T(8,128)(2,1)} async-done(((bf16[512,6144]{1,0:T(8,128)(2,1)}), bf16[32,6144]{1,0:T(8,128)(2,1)}) %reduce-scatter.3.cloned.1.call-update) | async-done | bytes 393232 | tf_op jit(solution)/shard_map/reduce_scatter | solution.py:28
  261.9 0.0 copy-done
  261.9 0.0 copy-done.3
  261.9 1.5 fusion.26
  263.4 83.1 %psum.7 = f32[6144]{0:T(1024)S(1)} all-reduce(f32[6144]{0:T(1024)S(1)} %get-tuple-element.3), channel_id=1, replica_groups=mesh['dp'=16,'tensor'=16] {'dp','tensor'}, use_global_device_ids=true, to_apply=%region_7.0 | all-reduce | flops 6144 | bytes 49152 | tf_op jit(solution)/shard_map/psum | solution.py:37
  346.5 0.6 broadcast_multiply_fusion
  347.1 0.0 copy-done.2
  347.1 2.1 fusion.23
  349.2 29.7 %reduce-scatter.5.cloned.1.call-done = bf16[384,768]{1,0:T(8,128)(2,1)} async-done(((bf16[6144,768]{1,0:T(8,128)(2,1)}), bf16[384,768]{1,0:T(8,128)(2,1)}) %reduce-scatter.5.cloned.1.call-update) | async-done | bytes 589840 | tf_op jit(solution)/shard_map/reduce_scatter | solution.py:48
  378.9 2.2 convert_multiply_fusion.2
  (4 shorter events, 0.0 us)
Async XLA Ops:
  7.2 254.8 %reduce-scatter.3.cloned.1.call-start = ((), (), s32[]{:S(2)}) async-start(), calls=%async_computation.3 | async-start | bytes 6684672 | tf_op jit(solution)/shard_map/reduce_scatter | solution.py:28
  10.9 152.4 %slice-start = ((s8[9437184]{0:T(1024)(128)(4,1)}), s8[4194304]{0:T(1024)(128)(4,1)S(1)}, s32[]{:S(2)}) async-start(s8[9437184]{0:T(1024)(128)(4,1)} %bitcast.7), calls=%async_computation.5 | async-start | bytes 8388608
  10.9 152.4 %slice-start.1 = ((s8[9437184]{0:T(1024)(128)(4,1)}), s8[4194304]{0:T(1024)(128)(4,1)S(1)}, s32[]{:S(2)}) async-start(s8[9437184]{0:T(1024)(128)(4,1)} %bitcast.7), calls=%async_computation.6 | async-start | bytes 8388608
  11.6 151.6 %slice-start.2 = ((s8[9437184]{0:T(1024)(128)(4,1)}), s8[1048576]{0:T(1024)(128)(4,1)S(1)}, s32[]{:S(2)}) async-start(s8[9437184]{0:T(1024)(128)(4,1)} %bitcast.7), calls=%async_computation.7 | async-start | bytes 2097152
  160.6 2.6 copy-start.1
  163.2 5.1 %copy-start.4 = (bf16[512,768]{1,0:T(8,128)(2,1)S(1)}, bf16[512,768]{1,0:T(8,128)(2,1)}, u32[]{:S(2)}) copy-start(bf16[512,768]{1,0:T(8,128)(2,1)} %param.8) | copy-start | bytes 2359300
  176.9 202.0 %reduce-scatter.5.cloned.1.call-start = ((), (), s32[]{:S(2)}) async-start(), calls=%async_computation.4 | async-start | bytes 10027008 | tf_op jit(solution)/shard_map/reduce_scatter | solution.py:48
  188.2 73.7 %copy-start = (bf16[32,6144]{1,0:T(8,128)(2,1)S(1)}, bf16[32,6144]{1,0:T(8,128)(2,1)}, u32[]{:S(2)}) copy-start(bf16[32,6144]{1,0:T(8,128)(2,1)} %param.5) | copy-start | bytes 1179652
  188.2 73.7 %copy-start.3 = (f32[6144]{0:T(1024)S(1)}, f32[6144]{0:T(1024)}, u32[]{:S(2)}) copy-start(f32[6144]{0:T(1024)} %param.6) | copy-start | bytes 73732
  188.2 158.9 %copy-start.2 = (bf16[32,6144]{1,0:T(8,128)(2,1)S(1)}, bf16[32,6144]{1,0:T(8,128)(2,1)}, u32[]{:S(2)}) copy-start(bf16[32,6144]{1,0:T(8,128)(2,1)} %param.9) | copy-start | bytes 1179652
Sparse Core Ops, SparseCore 0:
  177.0 84.8 reduce-scatter.2
  266.6 112.2 reduce-scatter.4

commit v2 on v0

--- a/solution.py
+++ b/solution.py
@@ -32,7 +32,7 @@
         tiled=True,
     ).astype(jnp.float32)
     scale_terms = jnp.sum(normed_gradient * standardized_input, axis=0)
-    scale_gradient = lax.psum(scale_terms, ("dp", "tensor")) / replicas
+    scale_gradient = jnp.sum(lax.all_gather(scale_terms, ("dp", "tensor")), axis=0) / replicas
     scaled_gradient = normed_gradient * gain
     first_average = jnp.mean(scaled_gradient, axis=1, keepdims=True)
     second_average = jnp.mean(scaled_gradient * standardized_input, axis=1, keepdims=True)

time: 328 us -> 1060 us (3.23)
  waiting for transfers between devices: 188 us -> 982 us
  blocking collectives: 83.6 us -> 0 us
    all_gather x0 -> x1, waiting for transfers between devices: none -> 712 us  [on_device(): lax.all_gather(scale_terms, ('dp', 'tensor'))]
    psum x1 -> x0, blocking collectives: 83.6 us -> none  [on_device(): scale_gradient = lax.psum(scale_terms, ('dp', 'tensor')) / replicas]
    reduce_scatter x1, waiting for transfers between devices: 29.3 us -> 112 us  [on_device(): lax.psum_scatter(term.astype(jnp.bfloat16), 'dp', scatter_dimension=0, ti...]
  transfers between devices with their start and end apart: 3 -> 4, of which waited for: 3 -> 4; matrix products, arithmetic and copies ran while one was open for 5% -> 2% of each run, Pallas kernels for 0% -> 0%
where the time goes in v2:
time: 1060 us; the launch traced here: 1050 us
  waiting for transfers between devices  982 us (93%)
  matrix products  32 us (3%)
  other arithmetic  14.3 us (1%)
  between operations  13.8 us (1%)
    all_gather x1, waiting for transfers between devices, on_device(): lax.all_gather(scale_terms, ('dp', 'tensor'))  712 us
    reduce_scatter x1, waiting for transfers between devices, on_device(): lax.psum_scatter(term.astype(jnp.bfloat16), 'dp', scatter_dimension=0, ti...  112 us
    all_gather x1, waiting for transfers between devices, on_device(): full = lax.all_gather(normed_output, 'tensor', axis=0, tiled=True)  85.2 us
    reduce_scatter x1, waiting for transfers between devices, on_device(): lax.psum_scatter(lax.dot_general(dpre, w_in, (((1,), (1,)), ((), ())), pr...  72.9 us
  transfers between devices with their start and end apart: 4, of which 4 were waited for; matrix products, arithmetic and copies ran while one was open for 2% of the time, Pallas kernels for 0%

profile of v2, /device:TPU:2, one launch (start us, length us, event | category | flops | bytes accessed | tf_op | source)
XLA Modules:
  0.0 1049.9 jit_solution(13652629415884180098)
XLA Ops:
  7.2 0.0 all-gather.4.cloned.1.call-start
  7.2 1.2 convert_reduce_fusion
  8.4 1.3 fusion.24
  9.7 1.9 fusion.19
  11.6 0.0 all-gather.4.cloned.1.call-update
  11.6 0.0 copy-start.3
  11.6 0.0 reduce-scatter.3.cloned.1.call-start
  11.7 85.2 %all-gather.4.cloned.1.call-done = bf16[512,6144]{1,0:T(8,128)(2,1)} async-done(((bf16[32,6144]{1,0:T(8,128)(2,1)}), bf16[512,6144]{1,0:T(8,128)(2,1)}) %all-gather.4.cloned.1.call-update) | async-done | bytes 6291472 | tf_op jit(solution)/shard_map/all_gather | solution.py:22
  96.9 9.3 fusion.51
  106.3 0.0 copy-done.3
  106.3 11.4 %convolution_convert_fusion.1 = bf16[512,6144]{1,0:T(8,128)(2,1)} fusion(bf16[6144,768]{1,0:T(8,128)(2,1)} %param.7, bf16[512,768]{1,0:T(8,128)(2,1)S(1)} %copy-done.3, f32[512,768]{1,0:T(8,128)S(1)} %fusion.51), kind=kOutput, calls=%fused_computation.1 | convolution fusion | flops 4843241472 | bytes 18087936 | tf_op jit(solution)/shard_map/dot_general | solution.py:27
  117.7 0.0 reduce-scatter.3.cloned.1.call-update
  117.7 0.0 reduce-scatter.5.cloned.1.call-start
  117.7 11.3 %convolution_convert_fusion = bf16[6144,768]{1,0:T(8,128)(2,1)} fusion(bf16[512,6144]{1,0:T(8,128)(2,1)} %all-gather.4.cloned.1.call-done, bf16[512,768]{1,0:T(8,128)(2,1)S(1)} %copy-done.3, f32[512,768]{1,0:T(8,128)S(1)} %fusion.51), kind=kOutput, calls=%fused_computation | convolution fusion | flops 4844814336 | bytes 18087936 | tf_op jit(solution)/shard_map/dot_general | solution.py:8
  129.0 0.0 copy-start
  129.0 0.0 copy-start.2
  129.0 0.0 copy-start.1
  129.0 0.0 reduce-scatter.5.cloned.1.call-update
  129.1 0.0 all-gather.6.cloned.1.call-start
  129.1 72.9 %reduce-scatter.3.cloned.1.call-done = bf16[32,6144]{1,0:T(8,128)(2,1)} async-done(((bf16[512,6144]{1,0:T(8,128)(2,1)}), bf16[32,6144]{1,0:T(8,128)(2,1)}) %reduce-scatter.3.cloned.1.call-update) | async-done | bytes 393232 | tf_op jit(solution)/shard_map/reduce_scatter | solution.py:26
  202.0 0.0 copy-done
  202.0 0.0 copy-done.2
  202.0 2.0 fusion.26
  204.0 0.0 all-gather.6.cloned.1.call-update
  204.0 0.0 copy-done.1
  204.0 2.1 fusion.23
  206.1 112.4 %reduce-scatter.5.cloned.1.call-done = bf16[384,768]{1,0:T(8,128)(2,1)} async-done(((bf16[6144,768]{1,0:T(8,128)(2,1)}), bf16[384,768]{1,0:T(8,128)(2,1)}) %reduce-scatter.5.cloned.1.call-update) | async-done | bytes 589840 | tf_op jit(solution)/shard_map/reduce_scatter | solution.py:46
  318.5 2.2 convert_multiply_fusion.2
  320.7 711.7 %all-gather.6.cloned.1.call-done = f32[1572864]{0:T(1024)} async-done(((f32[6144]{0:T(1024)}), f32[1572864]{0:T(1024)}) %all-gather.6.cloned.1.call-update) | async-done | bytes 6291472 | tf_op jit(solution)/shard_map/all_gather | solution.py:35
  1032.3 7.3 reshape.27
  1039.7 3.1 reduce_sum.59
  1042.8 0.6 broadcast_multiply_fusion
  (3 shorter events, 0.0 us)
Async XLA Ops:
  7.2 89.8 %all-gather.4.cloned.1.call-start = ((), (), s32[]{:S(2)}) async-start(), calls=%async_computation.2 | async-start | bytes 6684672 | tf_op jit(solution)/shard_map/all_gather | solution.py:22
  11.6 94.6 %copy-start.3 = (bf16[512,768]{1,0:T(8,128)(2,1)S(1)}, bf16[512,768]{1,0:T(8,128)(2,1)}, u32[]{:S(2)}) copy-start(bf16[512,768]{1,0:T(8,128)(2,1)} %param.8) | copy-start | bytes 2359300
  11.6 190.4 %reduce-scatter.3.cloned.1.call-start = ((), (), s32[]{:S(2)}) async-start(), calls=%async_computation.3 | async-start | bytes 6684672 | tf_op jit(solution)/shard_map/reduce_scatter | solution.py:26
  117.7 200.8 %reduce-scatter.5.cloned.1.call-start = ((), (), s32[]{:S(2)}) async-start(), calls=%async_computation.4 | async-start | bytes 10027008 | tf_op jit(solution)/shard_map/reduce_scatter | solution.py:46
  129.0 73.0 %copy-start = (bf16[32,6144]{1,0:T(8,128)(2,1)S(1)}, bf16[32,6144]{1,0:T(8,128)(2,1)}, u32[]{:S(2)}) copy-start(bf16[32,6144]{1,0:T(8,128)(2,1)} %param.5) | copy-start | bytes 1179652
  129.0 73.0 %copy-start.2 = (f32[6144]{0:T(1024)S(1)}, f32[6144]{0:T(1024)}, u32[]{:S(2)}) copy-start(f32[6144]{0:T(1024)} %param.6) | copy-start | bytes 73732
  129.0 75.0 %copy-start.1 = (bf16[32,6144]{1,0:T(8,128)(2,1)S(1)}, bf16[32,6144]{1,0:T(8,128)(2,1)}, u32[]{:S(2)}) copy-start(bf16[32,6144]{1,0:T(8,128)(2,1)} %param.9) | copy-start | bytes 1179652
  129.1 903.3 %all-gather.6.cloned.1.call-start = ((), (), s32[]{:S(2)}) async-start(), calls=%async_computation.5 | async-start | bytes 6316032 | tf_op jit(solution)/shard_map/all_gather | solution.py:35
Sparse Core Ops, SparseCore 0:
  11.7 85.1 all-gather.3
  117.8 84.1 reduce-scatter.2
  206.8 111.7 reduce-scatter.4
  320.8 711.4 all-gather.5
